TPU v7x, 512 devices: a whole 4x8x8 slice. The times are simulated.
512 devices in a mesh: tm: 4 (over y_hi, core), pix: 128 (over x, z, y_lo).
Axes of the slice: x: 4, y: 8 (y_hi: 2, y_lo: 4; y = y_hi * 4 + y_lo), z: 8, core: 2. Of those that a mesh axis runs over, the one named last changes fastest.
Arguments:
- activations: bfloat16 [4, 327680, 256], P('tm', 'pix'), may hold values from -6 to 6
- down_weight: bfloat16 [1024, 256], replicated, may hold values from -0.1875 to 0.1875
- down_bias: float32 [256], replicated, may hold values from -3 to 3
- taps: float32 [9, 256], replicated, may hold values from -2 to 2
- point_weight: bfloat16 [256, 256], replicated, may hold values from -0.375 to 0.375
- time_mix: float32 [4, 4, 256], replicated, may hold values from -3 to 3
- edge_rows: int32 [128, 2, 20], P('pix'), may hold values from 0 to 19, as said below
- cotangent: bfloat16 [4, 81920, 256], P(None, ('pix', 'tm')), may hold values from -6 to 6
Outputs:
- grad_input: bfloat16 [4, 327680, 256], P('tm', 'pix')
- grad_down: float32 [1024, 256], replicated
- grad_bias: float32 [256], replicated
- grad_taps: float32 [9, 256], replicated
- grad_point: float32 [256, 256], replicated
- grad_mix: float32 [4, 4, 256], replicated
Inputs may be any that keep to these rules, and one draw needn't show every extreme that they name: Each edge_rows[t, e] is either 0, 1, .., 19 or its reversal; edge_rows[t, 1] equals edge_rows[(t + 1) mod 128, 0].
All inputs are finite; a program needn't handle non-finite values.
Results may differ from a plain program's by a relative error of at most 0.014.
Values may be sent and summed in bfloat16 or wider, within the bound.
No kernel may reach another device: no remote copies, remote signals or barrier semaphores. Data moves between devices by JAX's collectives and lax.ppermute only.
A program may use at most 64 MiB of HBM per device.

v0:
```python
import math
import jax
import jax.numpy as jnp
from jax import lax
from jax.sharding import PartitionSpec as P

C = 256
TR = 20
TC = 32


def padded_2(cells, sides, width):
    for axis, dim in sides:
        count = lax.axis_size(axis)
        head = lax.slice_in_dim(cells, 0, width, axis=dim)
        tail = lax.slice_in_dim(cells, cells.shape[dim] - width, cells.shape[dim], axis=dim)
        cells = jnp.concatenate(
            [
                lax.ppermute(tail, axis, [(i, (i + 1) % count) for i in range(count)]),
                cells,
                lax.ppermute(head, axis, [((i + 1) % count, i) for i in range(count)]),
            ],
            axis=dim,
        )
    return cells


def on_device(
    activations, down_weight, down_bias, taps, point_weight, time_mix, edge_rows, cotangent
):
    frames = lax.axis_size("tm")
    tiles = lax.axis_size("pix")
    pixels = TR * TC
    scale = 1.0 / math.sqrt(frames * tiles * pixels)
    rows_in = activations.reshape(pixels, 4 * C)
    preact = jnp.dot(rows_in, down_weight, preferred_element_type=jnp.float32) + down_bias
    pooled = jax.nn.silu(preact).astype(jnp.bfloat16)
    tile_grid = pooled.reshape(1, TR, TC, C)
    padded = padded_2(tile_grid, (("pix", 2),), 1)
    west_map = edge_rows[0, 0]
    east_map = edge_rows[0, 1]
    west_col = jnp.take(padded[0, :, 0, :], west_map, axis=0)
    east_col = jnp.take(padded[0, :, TC + 1, :], east_map, axis=0)
    widened = jnp.concatenate([west_col[:, None, :], tile_grid[0], east_col[:, None, :]], axis=1)
    widened = jnp.pad(widened, ((1, 1), (0, 0), (0, 0)))
    spread = jnp.zeros((TR, TC, C), jnp.float32)
    for row_off in range(3):
        for col_off in range(3):
            spread = (
                spread
                + taps[row_off * 3 + col_off]
                * widened[row_off : row_off + TR, col_off : col_off + TC, :]
            )
    spread_low = spread.astype(jnp.bfloat16).reshape(pixels, C)
    mixed_in = (
        pooled.astype(jnp.float32)
        + jnp.dot(spread_low, point_weight, preferred_element_type=jnp.float32)
    ).astype(jnp.bfloat16)
    by_pixel = lax.all_to_all(
        mixed_in.reshape(1, pixels, C), "tm", split_axis=1, concat_axis=0, tiled=True
    )
    mix_part = jnp.einsum("gpc,fpc->fgc", by_pixel, cotangent, preferred_element_type=jnp.float32)
    cot_f = cotangent.astype(jnp.float32)
    mixed_acc = jnp.zeros((frames, cotangent.shape[1], C), jnp.float32)
    for source in range(frames):
        mixed_acc = mixed_acc + time_mix[source][:, None, :] * cot_f[source][None, :, :]
    mixed_grad = mixed_acc.astype(jnp.bfloat16)
    back_grad = lax.all_to_all(mixed_grad, "tm", split_axis=0, concat_axis=1, tiled=True)
    mixed_rows = back_grad.reshape(pixels, C)
    point_part = jnp.dot(spread_low.T, mixed_rows, preferred_element_type=jnp.float32)
    spread_grad = jnp.dot(mixed_rows, point_weight.T, preferred_element_type=jnp.float32).astype(
        jnp.bfloat16
    )
    grad_float = spread_grad.reshape(TR, TC, C).astype(jnp.float32)
    taps_rows = []
    for row_off in range(3):
        for col_off in range(3):
            taps_rows.append(
                jnp.sum(
                    grad_float * widened[row_off : row_off + TR, col_off : col_off + TC, :],
                    axis=(0, 1),
                )
            )
    taps_part = jnp.stack(taps_rows, axis=0)
    grad_padded = jnp.pad(grad_float, ((2, 2), (2, 2), (0, 0)))
    wide_grad = jnp.zeros((TR + 2, TC + 2, C), jnp.float32)
    for row_off in range(3):
        for col_off in range(3):
            wide_grad = (
                wide_grad
                + taps[row_off * 3 + col_off]
                * grad_padded[2 - row_off : 4 - row_off + TR, 2 - col_off : 4 - col_off + TC, :]
            )
    west_back = jnp.take(wide_grad[1 : TR + 1, 0, :], west_map, axis=0)
    east_back = jnp.take(wide_grad[1 : TR + 1, TC + 1, :], east_map, axis=0)
    outgoing = jnp.stack([west_back, east_back], axis=1)
    incoming = padded_2(outgoing.astype(jnp.bfloat16), (("pix", 1),), 1).astype(outgoing.dtype)
    inner_grad = wide_grad[1 : TR + 1, 1 : TC + 1, :]
    inner_grad = inner_grad.at[:, 0, :].add(incoming[:, 0, :])
    inner_grad = inner_grad.at[:, TC - 1, :].add(incoming[:, 3, :])
    pooled_grad = mixed_rows.astype(jnp.float32) + inner_grad.reshape(pixels, C)
    sigma = jax.nn.sigmoid(preact)
    pre_grad = (pooled_grad * (sigma * (1.0 + preact * (1.0 - sigma)))).astype(jnp.bfloat16)
    bias_part = jnp.sum(pre_grad.astype(jnp.float32), axis=0)
    down_part = jnp.dot(rows_in.T, pre_grad, preferred_element_type=jnp.float32)
    grad_input = jnp.dot(pre_grad, down_weight.T, preferred_element_type=jnp.float32).astype(
        jnp.bfloat16
    )
    terms = (
        down_part,
        point_part,
        taps_part,
        mix_part.reshape(frames * frames, C),
        bias_part.reshape(1, C),
    )
    totals = lax.psum((terms[0], terms[1], terms[2], terms[3], terms[4]), ("tm", "pix"))
    grad_down = totals[0] * scale
    grad_point = totals[1] * scale
    grad_taps = totals[2] * scale
    grad_mix = totals[3].reshape(frames, frames, C) * scale
    grad_bias = totals[4].reshape(C) * scale
    return (
        grad_input.reshape(1, 4 * pixels, C),
        grad_down,
        grad_bias,
        grad_taps,
        grad_point,
        grad_mix,
    )


def solution(mesh):
    in_specs = (
        P("tm", "pix", None),
        P(),
        P(),
        P(),
        P(),
        P(),
        P("pix", None, None),
        P(None, ("pix", "tm"), None),
    )
    out_specs = (P("tm", "pix", None), P(), P(), P(), P(), P())
    return jax.shard_map(
        on_device, mesh=mesh, in_specs=in_specs, out_specs=out_specs, check_vma=False
    )
```

profile of v0, /device:TPU:24, one launch (start us, length us, event | category | flops | bytes accessed | tf_op | source)
XLA Modules:
  0.0 374.9 jit_solution(8974585061847904464)
XLA Ops:
  7.2 0.8 slice_bitcast_fusion.9
  8.0 1.0 convert_element_type.87
  9.1 0.9 add_convert_fusion
  10.0 4.4 %all-to-all-start = ((bf16[4,160,256]{2,1,0:T(8,128)(2,1)}), bf16[4,160,256]{2,1,0:T(8,128)(2,1)S(1)}, u32[]{:S(2)}, u32[]{:S(2)}) async-start(bf16[4,160,256]{2,1,0:T(8,128)(2,1)} %add_convert_fusion), calls=%async_computation | async-start | bytes 655360 | tf_op jit(solution)/shard_map/all_to_all | solution.py:68
  14.5 10.7 %all-to-all-done = bf16[4,160,256]{2,1,0:T(8,128)(2,1)S(1)} async-done(((bf16[4,160,256]{2,1,0:T(8,128)(2,1)}), bf16[4,160,256]{2,1,0:T(8,128)(2,1)S(1)}, u32[]{:S(2)}, u32[]{:S(2)}) %all-to-all-start) | async-done | bytes 327712 | tf_op jit(solution)/shard_map/all_to_all | solution.py:68
  26.4 0.9 copy-done.1
  28.0 6.7 %collective-permute-start.1 = (bf16[20,1,256]{2,0,1:T(8,128)(2,1)S(1)}, bf16[20,1,256]{2,0,1:T(8,128)(2,1)S(1)}, u32[]{:S(2)}, u32[]{:S(2)}) collective-permute-start(bf16[20,1,256]{2,0,1:T(8,128)(2,1)S(1)} %fusion.49), channel_id=1, source_target_pairs={{1,0},{2,1},{3,2},{4,3},{5,4},{6,5},{7,6},{8,7},{9,8},{10,9},{11,1... | collective-permute-start | bytes 30728 | tf_op jit(solution)/shard_map/ppermute | solution.py:21
  35.4 1.9 collective-permute-start
  37.3 1.1 copy.60
  38.4 2.5 reshape.139
  40.9 1.2 slice.257
  42.1 0.7 fusion.47
  43.1 0.8 fusion.34
  43.9 1.6 convolution_bitcast_fusion
  45.5 3.9 %collective-permute-start.3 = (bf16[1,20,1,256]{3,1,2,0:T(8,128)(2,1)S(1)}, bf16[1,20,1,256]{3,1,2,0:T(8,128)(2,1)S(1)}, u32[]{:S(2)}, u32[]{:S(2)}) collective-permute-start(bf16[1,20,1,256]{3,1,2,0:T(8,128)(2,1)S(1)} %copy.65), channel_id=1, source_target_pairs={{1,0},{2,1},{3,2},{4,3},{5,4},{6,5},{7,6},{8,7},{9,8},{10,9},{11,1... | collective-permute-start | bytes 30728 | tf_op jit(solution)/shard_map/ppermute | solution.py:21
  49.4 4.6 %collective-permute-start.2 = (bf16[1,20,1,256]{3,1,2,0:T(8,128)(2,1)S(1)}, bf16[1,20,1,256]{3,1,2,0:T(8,128)(2,1)S(1)}, u32[]{:S(2)}, u32[]{:S(2)}) collective-permute-start(bf16[1,20,1,256]{3,1,2,0:T(8,128)(2,1)S(1)} %copy.64), channel_id=1, source_target_pairs={{0,1},{1,2},{2,3},{3,4},{4,5},{5,6},{6,7},{7,8},{8,9},{9,10},{10,1... | collective-permute-start | bytes 30728 | tf_op jit(solution)/shard_map/ppermute | solution.py:19
  54.6 1.6 reshape.140
  56.9 1.8 collective-permute-done.2
  59.6 0.8 fusion.30
  61.6 3.4 reduce.5
  65.0 1.8 reshape.191
  66.8 3.5 all-to-all-start.1
  70.3 1.0 fusion.53
  71.3 0.7 fusion.38
  72.1 8.8 %all-to-all-done.1 = bf16[4,2,20480]{2,1,0:T(2,128)(2,1)S(1)} async-done(((bf16[4,2,20480]{2,1,0:T(2,128)(2,1)}), bf16[4,2,20480]{2,1,0:T(2,128)(2,1)S(1)}, u32[]{:S(2)}, u32[]{:S(2)}) %all-to-all-start.1) | async-done | bytes 327712 | tf_op jit(solution)/shard_map/all_to_all | solution.py:59
  82.2 108.8 %all-reduce.2 = (f32[1,256]{1,0:T(1,128)S(1)}, f32[9,256]{1,0:T(8,128)S(1)}, f32[16,256]{1,0:T(8,128)S(1)}) all-reduce(f32[1,256]{1,0:T(1,128)S(1)} %bitcast.136, f32[9,256]{1,0:T(8,128)S(1)} %stack.51, f32[16,256]{1,0:T(8,128)S(1)} %reshape.145), channel_id=1, replica_groups=mesh['tm'=4,'pix'=128] {'tm','pix'}, use_global_device_ids=true, to_apply=%region_2.4 | all-reduce | flops 6656 | bytes 53248 | tf_op jit(solution)/shard_map/psum | solution.py:116
  191.0 0.6 mul.396
  192.2 0.6 broadcast_multiply_fusion.3
  192.8 171.9 %all-reduce.6.cloned.1.call-done = (f32[1024,256]{0,1:T(8,128)}, f32[256,256]{1,0:T(8,128)}) async-done(((f32[1024,256]{0,1:T(8,128)}, f32[256,256]{1,0:T(8,128)}), (f32[1024,256]{0,1:T(8,128)}, f32[256,256]{1,0:T(8,128)})) %all-reduce.6.cloned.1.call-update) | async-done | bytes 1310736 | tf_op jit(solution)/shard_map/psum | solution.py:116
  364.6 1.3 broadcast_multiply_fusion
  366.0 1.3 copy.62
  367.3 0.7 broadcast_multiply_fusion.1
  (59 shorter events, 8.3 us)
Async XLA Ops:
  7.2 35.9 %copy-start = (bf16[1024,256]{1,0:T(8,128)(2,1)S(1)}, bf16[1024,256]{1,0:T(8,128)(2,1)}, u32[]{:S(2)}) copy-start(bf16[1024,256]{1,0:T(8,128)(2,1)} %param.17) | copy-start | bytes 1572868
  9.0 5.4 %copy-start.7 = (s32[1,2,20]{2,1,0:T(2,128)S(1)}, s32[1,2,20]{2,1,0:T(2,128)}, u32[]{:S(2)}) copy-start(s32[1,2,20]{2,1,0:T(2,128)} %param.22) | copy-start | bytes 484
  9.0 5.4 %copy-start.6 = (f32[9,256]{1,0:T(8,128)S(1)}, f32[9,256]{1,0:T(8,128)}, u32[]{:S(2)}) copy-start(f32[9,256]{1,0:T(8,128)} %param.19) | copy-start | bytes 27652
  9.0 16.1 %copy-start.3 = (bf16[256,256]{1,0:T(8,128)(2,1)S(1)}, bf16[256,256]{1,0:T(8,128)(2,1)}, u32[]{:S(2)}) copy-start(bf16[256,256]{1,0:T(8,128)(2,1)} %param.20) | copy-start | bytes 393220
  10.0 15.1 %all-to-all-start = ((bf16[4,160,256]{2,1,0:T(8,128)(2,1)}), bf16[4,160,256]{2,1,0:T(8,128)(2,1)S(1)}, u32[]{:S(2)}, u32[]{:S(2)}) async-start(bf16[4,160,256]{2,1,0:T(8,128)(2,1)} %add_convert_fusion), calls=%async_computation | async-start | bytes 655360 | tf_op jit(solution)/shard_map/all_to_all | solution.py:68
  25.8 11.5 %copy-start.2 = (bf16[4,160,256]{2,1,0:T(8,128)(2,1)S(1)}, bf16[4,160,256]{2,1,0:T(8,128)(2,1)}, u32[]{:S(2)}) copy-start(bf16[4,160,256]{2,1,0:T(8,128)(2,1)} %param.23) | copy-start | bytes 983044
  26.4 0.9 copy-start.1
  28.0 14.1 %collective-permute-start.1 = (bf16[20,1,256]{2,0,1:T(8,128)(2,1)S(1)}, bf16[20,1,256]{2,0,1:T(8,128)(2,1)S(1)}, u32[]{:S(2)}, u32[]{:S(2)}) collective-permute-start(bf16[20,1,256]{2,0,1:T(8,128)(2,1)S(1)} %fusion.49), channel_id=1, source_target_pairs={{1,0},{2,1},{3,2},{4,3},{5,4},{6,5},{7,6},{8,7},{9,8},{10,9},{11,1... | collective-permute-start | bytes 30728 | tf_op jit(solution)/shard_map/ppermute | solution.py:21
  35.4 6.7 %collective-permute-start = (bf16[20,1,256]{2,0,1:T(8,128)(2,1)S(1)}, bf16[20,1,256]{2,0,1:T(8,128)(2,1)S(1)}, u32[]{:S(2)}, u32[]{:S(2)}) collective-permute-start(bf16[20,1,256]{2,0,1:T(8,128)(2,1)S(1)} %fusion.48), channel_id=1, source_target_pairs={{0,1},{1,2},{2,3},{3,4},{4,5},{5,6},{6,7},{7,8},{8,9},{9,10},{10,1... | collective-permute-start | bytes 30728 | tf_op jit(solution)/shard_map/ppermute | solution.py:19
  40.9 2.2 copy-start.8
  45.5 10.7 %collective-permute-start.3 = (bf16[1,20,1,256]{3,1,2,0:T(8,128)(2,1)S(1)}, bf16[1,20,1,256]{3,1,2,0:T(8,128)(2,1)S(1)}, u32[]{:S(2)}, u32[]{:S(2)}) collective-permute-start(bf16[1,20,1,256]{3,1,2,0:T(8,128)(2,1)S(1)} %copy.65), channel_id=1, source_target_pairs={{1,0},{2,1},{3,2},{4,3},{5,4},{6,5},{7,6},{8,7},{9,8},{10,9},{11,1... | collective-permute-start | bytes 30728 | tf_op jit(solution)/shard_map/ppermute | solution.py:21
  49.4 9.2 %collective-permute-start.2 = (bf16[1,20,1,256]{3,1,2,0:T(8,128)(2,1)S(1)}, bf16[1,20,1,256]{3,1,2,0:T(8,128)(2,1)S(1)}, u32[]{:S(2)}, u32[]{:S(2)}) collective-permute-start(bf16[1,20,1,256]{3,1,2,0:T(8,128)(2,1)S(1)} %copy.64), channel_id=1, source_target_pairs={{0,1},{1,2},{2,3},{3,4},{4,5},{5,6},{6,7},{7,8},{8,9},{9,10},{10,1... | collective-permute-start | bytes 30728 | tf_op jit(solution)/shard_map/ppermute | solution.py:19
  66.8 14.1 %all-to-all-start.1 = ((bf16[4,2,20480]{2,1,0:T(2,128)(2,1)}), bf16[4,2,20480]{2,1,0:T(2,128)(2,1)S(1)}, u32[]{:S(2)}, u32[]{:S(2)}) async-start(bf16[4,2,20480]{2,1,0:T(2,128)(2,1)} %reshape.191), calls=%async_computation.1 | async-start | bytes 655360 | tf_op jit(solution)/shard_map/all_to_all | solution.py:59
  70.2 294.4 %all-reduce.6.cloned.1.call-start = ((), (), s32[]{:S(2)}) async-start(), calls=%async_computation.2 | async-start | bytes 2621440 | tf_op jit(solution)/shard_map/psum | solution.py:116
  72.1 9.5 %copy-start.4 = (bf16[4,160,256]{1,0,2:T(4,128)(2,1)S(1)}, bf16[4,160,256]{1,0,2:T(4,128)(2,1)}, u32[]{:S(2)}) copy-start(bf16[4,160,256]{1,0,2:T(4,128)(2,1)} %copy.60) | copy-start | bytes 983044
  366.0 1.3 copy-start.5
Sparse Core Ops, SparseCore 0:
  76.7 287.8 all-reduce.5
where the time goes:
time: 376 us; the launch traced here: 375 us
  waiting for transfers between devices  193 us (51%)
  blocking collectives  109 us (29%)
  starting transfers between devices  25 us (7%)
  local copies, waits for them, and re-layouts  17 us (5%)
  between operations  14.4 us (4%)
  other arithmetic  11.8 us (3%)
  matrix products  4.79 us (1%)
    psum x1, waiting for transfers between devices, on_device(): lax.psum((terms[0], terms[1], terms[2], terms[3], terms[4]), ('tm', 'pix'))  172 us
    psum x1, blocking collectives, on_device(): lax.psum((terms[0], terms[1], terms[2], terms[3], terms[4]), ('tm', 'pix'))  109 us
    all_to_all x1, waiting for transfers between devices, on_device(): lax.all_to_all(mixed_grad, 'tm', split_axis=0, concat_axis=1, tiled=True)  10.7 us
    ppermute x2, starting transfers between devices, padded_2(): lax.ppermute(head, axis, [((i + 1) % count, i) for i in range(count)])  10.6 us
    all_to_all x1, waiting for transfers between devices, on_device(): lax.all_to_all(mixed_in.reshape(1, pixels, C), 'tm', split_axis=1, concat...  8.76 us
  transfers between devices with their start and end apart: 7, of which 4 were waited for; matrix products, arithmetic and copies ran while one was open for 4% of the time, Pallas kernels for 0%

commit v1 on v0

--- a/solution.py
+++ b/solution.py
@@ -113,7 +113,9 @@
         mix_part.reshape(frames * frames, C),
         bias_part.reshape(1, C),
     )
-    totals = lax.psum((terms[0], terms[1], terms[2], terms[3], terms[4]), ("tm", "pix"))
+    tile_in = (terms[0], terms[1], terms[2], terms[3], terms[4])
+    part_next = lax.psum(tile_in, "pix")
+    totals = lax.psum(part_next, "tm")
     grad_down = totals[0] * scale
     grad_point = totals[1] * scale
     grad_taps = totals[2] * scale

time: 376 us -> 2170 us (5.77)
  the two profiles are of different devices: /device:TPU:24 before, /device:TPU:1 now
where the time goes in v1:
time: 2170 us
  waiting for transfers between devices  1270 us (59%)
  blocking collectives  815 us (38%)
  starting transfers between devices  37.1 us (2%)
    psum x1, waiting for transfers between devices, on_device(): part_next = lax.psum(tile_in, 'pix')  1250 us
    psum x1, blocking collectives, on_device(): part_next = lax.psum(tile_in, 'pix')  618 us
    psum x1, blocking collectives, on_device(): totals = lax.psum(part_next, 'tm')  197 us
  transfers between devices with their start and end apart: 8, of which 4 were waited for; matrix products, arithmetic and copies ran while one was open for 1% of the time, Pallas kernels for 0%

profile of v1, /device:TPU:1, one launch (start us, length us, event | category | flops | bytes accessed | tf_op | source)
XLA Modules:
  0.0 2172.9 jit_solution(5190396444174710127)
XLA Ops:
  7.2 0.8 slice_bitcast_fusion.9
  8.0 1.0 convert_element_type.87
  9.1 0.9 add_convert_fusion
  10.0 10.3 all-to-all-start
  20.4 9.8 all-to-all-done
  31.5 0.9 copy-done.1
  33.1 11.3 collective-permute-start.1
  45.1 1.9 collective-permute-start
  47.0 2.5 reshape.139
  49.5 1.2 slice.257
  50.7 4.8 collective-permute-done
  55.5 0.7 fusion.47
  56.5 0.8 fusion.34
  57.4 4.6 collective-permute-start.3
  62.0 1.9 collective-permute-start.2
  63.9 1.6 convolution_bitcast_fusion
  66.1 6.4 collective-permute-done.2
  73.4 0.8 fusion.30
  74.2 1.0 fusion.53
  75.2 1.1 copy.60
  77.5 2.7 reduce.5
  80.2 0.8 reshape.191
  81.1 7.0 all-to-all-start.1
  88.1 1251.8 %all-reduce.9.cloned.1.call-done = (f32[1024,256]{0,1:T(8,128)}, f32[256,256]{1,0:T(8,128)}) async-done(((f32[1024,256]{0,1:T(8,128)}, f32[256,256]{1,0:T(8,128)}), (f32[1024,256]{0,1:T(8,128)}, f32[256,256]{1,0:T(8,128)})) %all-reduce.9.cloned.1.call-update) | async-done | bytes 1310736 | tf_op jit(solution)/shard_map/psum | solution.py:117
  1339.9 1.5 convolution_convert_fusion
  1341.4 1.6 reshape.140
  1343.9 1.3 reshape.192
  1346.2 617.7 %all-reduce.2 = (f32[1,256]{1,0:T(1,128)S(1)}, f32[9,256]{1,0:T(8,128)S(1)}, f32[16,256]{1,0:T(8,128)S(1)}) all-reduce(f32[1,256]{1,0:T(1,128)S(1)} %bitcast.136, f32[9,256]{1,0:T(8,128)S(1)} %stack.51, f32[16,256]{1,0:T(8,128)S(1)} %reshape.145), channel_id=1, replica_groups=mesh['tm'=4,'pix'=128] {'pix'}, use_global_device_ids=true, to_apply=%region_3.5 | all-reduce | flops 6656 | bytes 53248 | tf_op jit(solution)/shard_map/psum | solution.py:117
  1963.8 197.1 %all-reduce.4 = (f32[1,256]{1,0:T(1,128)S(1)}, f32[9,256]{1,0:T(8,128)S(1)}, f32[16,256]{1,0:T(8,128)S(1)}) all-reduce(f32[1,256]{1,0:T(1,128)S(1)} %get-tuple-element.66, f32[9,256]{1,0:T(8,128)S(1)} %get-tuple-element.67, f32[16,256]{1,0:T(8,128)S(1)} %get-tuple-element.68), channel_id=1, replica_groups=mesh['tm'=4,'pix'=128] {'tm'}, use_global_device_ids=true, to_apply=%region_4.6 | all-reduce | flops 6656 | bytes 53248 | tf_op jit(solution)/shard_map/psum | solution.py:118
  2162.7 1.3 broadcast_multiply_fusion
  2164.0 1.3 copy.62
  2165.3 0.7 broadcast_multiply_fusion.1
  (65 shorter events, 9.4 us)
Async XLA Ops:
  7.2 49.3 %copy-start = (bf16[1024,256]{1,0:T(8,128)(2,1)S(1)}, bf16[1024,256]{1,0:T(8,128)(2,1)}, u32[]{:S(2)}) copy-start(bf16[1024,256]{1,0:T(8,128)(2,1)} %param.17) | copy-start | bytes 1572868
  9.0 11.3 copy-start.8
  9.0 11.3 copy-start.7
  9.0 21.2 copy-start.4
  10.0 20.2 all-to-all-start
  20.3 1319.6 %all-reduce.9.cloned.1.call-start = ((), (), s32[]{:S(2)}) async-start(), calls=%async_computation.2 | async-start | bytes 2621440 | tf_op jit(solution)/shard_map/psum | solution.py:117
  31.5 0.9 copy-start.1
  33.1 17.7 collective-permute-start.1
  45.1 10.4 collective-permute-start
  49.5 7.0 copy-start.9
  57.3 8.2 copy-start.3
  57.4 8.1 collective-permute-start.3
  62.0 10.5 collective-permute-start.2
  74.2 1.1 copy-start.2
  81.1 1262.8 %all-to-all-start.1 = ((bf16[4,2,20480]{2,1,0:T(2,128)(2,1)}), bf16[4,2,20480]{2,1,0:T(2,128)(2,1)}, u32[]{:S(2)}, u32[]{:S(2)}) async-start(bf16[4,2,20480]{2,1,0:T(2,128)(2,1)} %reshape.191), calls=%async_computation.1 | async-start | bytes 655360 | tf_op jit(solution)/shard_map/all_to_all | solution.py:59
  88.1 2074.6 %all-reduce.11.cloned.1.call-start = ((), (), s32[]{:S(2)}) async-start(), calls=%async_computation.3 | async-start | bytes 2621440 | tf_op jit(solution)/shard_map/psum | solution.py:118
  1343.8 1.7 copy-start.5
  2164.0 1.3 copy-start.6
Sparse Core Ops, SparseCore 0:
  75.3 1264.5 all-reduce.8
  1343.2 141.6 all-reduce.10
